TPU v7x, 32 devices: a whole 2x2x4 slice. The times are simulated.
32 devices in a mesh: view: 8 (over z, x), slab: 4 (over y, core).
Axes of the slice: x: 2, y: 2, z: 4, core: 2. Of those that a mesh axis runs over, the one named last changes fastest.
Arguments:
- volume: float32 [4, 128, 128], P('slab', 'view'), may hold values from 0 to 2
- tile_blocks: bfloat16 [8, 4, 192, 128, 128], P('view', 'slab'), may hold values from 0.0009994507 to 0.014953613
- pixel_tile: int32 [8, 4, 192], P('view', 'slab'), may hold values from 0 to 127, as said below
- ray_tile: int32 [8, 4, 192], P('view', 'slab'), may hold values from 0 to 127, as said below
- counts: int32 [8, 4], P('view', 'slab'), may hold values from 16 to 192, as said below
- subset_views: int32 [8, 4], P('view'), may hold values from 0 to 7, as said below
- sinogram: float32 [8, 128, 128], P('view', 'slab'), may hold values from 0 to 3
- weights: float32 [8, 128, 128], P('view', 'slab'), may hold values from 0.1 to 1
Outputs:
- updated: float32 [4, 128, 128], P('slab', 'view')
- denominators: float32 [4, 128, 128], P('slab', 'view')
Inputs may be any that keep to these rules, and one draw needn't show every extreme that they name: `counts`: for every group exactly one slab has 192 live slots; every count is at least 16. `pixel_tile`: slots k < 16 of group g name volume tiles g * 16 + k in every slab; slots at or past the count hold indices in range and are unused. `ray_tile`: slots at or past the count hold indices in range and are unused. `subset_views`: each group lists 4 distinct views in rising order.
All inputs are finite; a program needn't handle non-finite values.
Results may differ from a plain program's by a relative error of at most 0.00032.
Values may be sent and summed in bfloat16 or wider, within the bound.
No kernel may reach another device: no remote copies, remote signals or barrier semaphores. Data moves between devices by JAX's collectives and lax.ppermute only.
A program may use at most 64 MiB of HBM per device.

v0:
```python
import jax
import jax.numpy as jnp
from jax import lax
from jax.sharding import PartitionSpec as P

VG = 8
SUBSETS = 2


def make_ratio(totals, measured, weight, subset):
    ray_rows = jnp.arange(totals.shape[0], dtype=jnp.int32)
    view_of = ray_rows % VG
    in_subset = jnp.any(subset[None, :] == view_of[:, None], axis=1).astype(jnp.float32)
    denominator_rays = weight * totals[:, 1]
    residual_rays = in_subset[:, None] * weight * (measured - totals[:, 0])
    return jnp.stack([denominator_rays, residual_rays], axis=1).astype(jnp.bfloat16)


def on_device(volume, tile_blocks, pixel_tile, ray_tile, counts, subset_views, sinogram, weights):
    local_tiles = tile_blocks[0, 0]
    pixel_rows = pixel_tile[0, 0]
    ray_rows = ray_tile[0, 0]
    count_here = counts[0, 0]
    subset = subset_views[0]
    ray_total = sinogram.shape[1] * lax.axis_size("slab")
    voxel_total = volume.shape[1] * lax.axis_size("view")
    live_mask = (jnp.arange(local_tiles.shape[0], dtype=jnp.int32) < count_here).astype(jnp.float32)
    own_image = volume[0].astype(jnp.bfloat16)
    slab_image = lax.all_gather(own_image, "view", axis=0, tiled=True)
    picked = slab_image[pixel_rows]
    operand = jnp.stack([picked, jnp.ones_like(picked)], axis=1)
    products = jnp.einsum("krv,kcv->kcr", local_tiles, operand, preferred_element_type=jnp.float32)
    products = products * live_mask[:, None, None]
    partial_rays = jax.ops.segment_sum(products, ray_rows, num_segments=ray_total)
    measured, weight = (
        lax.all_gather(sinogram[0], "slab", axis=0, tiled=True),
        lax.all_gather(weights[0], "slab", axis=0, tiled=True),
    )
    totals = lax.psum(partial_rays, "slab")
    back_in = make_ratio(totals, measured, weight, subset)
    gathered = back_in[ray_rows]
    back_products = jnp.einsum(
        "krv,kcr->kcv", local_tiles, gathered, preferred_element_type=jnp.float32
    )
    back_products = back_products * live_mask[:, None, None]
    partial_voxels = jax.ops.segment_sum(back_products, pixel_rows, num_segments=voxel_total)
    voxel_share = lax.psum_scatter(partial_voxels, "view", scatter_dimension=0, tiled=True)
    denominators = voxel_share[:, 0, :]
    gradient = voxel_share[:, 1, :]
    updated = jnp.maximum(volume[0] + SUBSETS * gradient / denominators, 0.0)
    return (updated[None], denominators[None])


def solution(mesh):
    return jax.shard_map(
        on_device,
        mesh=mesh,
        in_specs=(
            P("slab", "view", None),
            P("view", "slab", None, None, None),
            P("view", "slab", None),
            P("view", "slab", None),
            P("view", "slab"),
            P("view", None),
            P("view", "slab", None),
            P("view", "slab", None),
        ),
        out_specs=(P("slab", "view", None), P("slab", "view", None)),
        check_vma=False,
    )
```

profile of v0, /device:TPU:0, one launch (start us, length us, event | category | flops | bytes accessed | tf_op | source)
XLA Modules:
  0.0 182.9 jit_solution(6079675270705240020)
XLA Ops:
  7.2 0.0 copy-start.6
  7.2 0.0 copy-start.8
  7.2 0.0 copy-start.4
  7.2 0.0 copy-start.5
  7.2 0.0 all-reduce.5.cloned.1.call-start
  7.9 0.7 convert_element_type.21
  8.6 32.4 %all-gather.1 = bf16[1,128,128]{2,1,0:T(8,128)(2,1)S(1)} all-gather(bf16[1,16,128]{2,1,0:T(8,128)(2,1)S(1)} %convert_element_type.21), channel_id=3, replica_groups=mesh['view'=8,'slab'=4] {'view'}, dimensions={1}, use_global_device_ids=true | all-gather | bytes 36864 | tf_op jit(solution)/shard_map/all_gather | solution.py:29
  41.0 0.7 compare_select_fusion.1
  41.7 0.8 gather_fusion
  42.5 0.1 copy.19
  42.6 0.0 copy-start.7
  42.6 6.1 %fusion.4 = f32[192,2,128]{2,1,0:T(2,128)S(1)} fusion(bf16[1,1,192,128,128]{4,3,2,1,0:T(8,128)(2,1)} %param.9, f32[192]{0:T(256)S(1)} %compare_convert_fusion, bf16[192,1,128]{2,1,0:T(2,128)(2,1)S(1)} %copy.19), kind=kOutput, calls=%fused_computation.8 | convolution fusion | flops 12632064 | bytes 6537984 | tf_op jit(solution)/shard_map/krv,kcv->kcr/dot_general | solution.py:32
  48.7 0.0 copy-start.9
  48.7 0.0 copy-start.2
  48.8 0.0 copy-done.6
  48.8 7.2 %scatter_fusion = f32[128,2,128]{2,1,0:T(2,128)S(1)} fusion(f32[128,2,128]{2,1,0:T(2,128)S(1)} %broadcast.74.clone, s32[192]{0:T(256)S(1)} %bitcast.68, f32[192,2,128]{2,1,0:T(2,128)S(1)} %fusion.4), kind=kCustom, calls=%fused_computation.2 | custom fusion | flops 49152 | bytes 590592 | tf_op jit(solution)/shard_map/scatter-add | solution.py:34
  55.9 0.0 copy-start.1
  56.0 0.6 copy-done.1
  56.6 0.0 all-reduce.5.cloned.1.call-update
  56.6 0.0 all-reduce.7.cloned.1.call-start
  56.7 0.0 copy-done.8
  56.7 0.1 compare_reduce_fusion
  56.8 0.0 copy-done.4
  56.8 5.2 %all-gather = f32[1,128,128]{2,1,0:T(8,128)S(1)} all-gather(f32[1,32,128]{2,1,0:T(8,128)S(1)} %copy-done.4), channel_id=2, replica_groups=mesh['view'=8,'slab'=4] {'slab'}, dimensions={1}, use_global_device_ids=true | all-gather | bytes 81920 | tf_op jit(solution)/shard_map/all_gather | solution.py:37
  62.0 0.0 copy-done.5
  62.1 5.2 %all-gather.2 = f32[1,128,128]{2,1,0:T(8,128)S(1)} all-gather(f32[1,32,128]{2,1,0:T(8,128)S(1)} %copy-done.5), channel_id=4, replica_groups=mesh['view'=8,'slab'=4] {'slab'}, dimensions={1}, use_global_device_ids=true | all-gather | bytes 81920 | tf_op jit(solution)/shard_map/all_gather | solution.py:36
  67.3 22.2 %all-reduce.5.cloned.1.call-done = f32[128,2,128]{2,1,0:T(2,128)} async-done(((f32[128,2,128]{2,1,0:T(2,128)}), f32[128,2,128]{2,1,0:T(2,128)}) %all-reduce.5.cloned.1.call-update) | async-done | bytes 131088 | tf_op jit(solution)/shard_map/psum | solution.py:39
  89.5 1.1 fusion.19
  90.5 0.1 fusion.14
  90.7 0.1 copy.21
  90.7 0.8 gather_fusion.1
  91.6 4.5 %fusion.7 = f32[192,2,128]{2,1,0:T(2,128)S(1)} fusion(bf16[192,2,128]{2,1,0:T(2,128)(2,1)S(1)} %gather_fusion.1, bf16[1,1,192,128,128]{4,3,2,1,0:T(8,128)(2,1)} %param.9, f32[192]{0:T(256)S(1)} %compare_convert_fusion), kind=kOutput, calls=%fused_computation.9 | convolution fusion | flops 12632064 | bytes 6587136 | tf_op jit(solution)/shard_map/krv,kcr->kcv/dot_general | solution.py:42
  96.1 0.0 copy-done.7
  96.2 7.1 %scatter_fusion.1 = f32[128,2,128]{2,1,0:T(2,128)S(1)} fusion(f32[128,2,128]{2,1,0:T(2,128)S(1)} %broadcast.74, s32[192]{0:T(256)S(1)} %bitcast.69, f32[192,2,128]{2,1,0:T(2,128)S(1)} %fusion.7), kind=kCustom, calls=%fused_computation.3 | custom fusion | flops 49152 | bytes 590592 | tf_op jit(solution)/shard_map/scatter-add | solution.py:46
  103.3 0.0 copy-start
  103.3 0.6 copy-done
  104.0 0.0 all-reduce.7.cloned.1.call-update
  104.0 0.0 copy-done.9
  104.0 0.6 dynamic-slice
  105.2 69.4 %all-reduce.7.cloned.1.call-done = f32[128,2,128]{2,1,0:T(2,128)} async-done(((f32[128,2,128]{2,1,0:T(2,128)}), f32[128,2,128]{2,1,0:T(2,128)}) %all-reduce.7.cloned.1.call-update) | async-done | bytes 131088
  174.6 0.8 constant_dynamic-slice_fusion
  175.4 0.0 copy-start.3
  175.5 0.0 copy-done.2
  175.5 0.6 fusion.17
  176.1 0.0 copy-done.3
  (9 shorter events, 0.1 us)
Async XLA Ops:
  7.2 41.6 %copy-start.6 = (s32[1,1,192]{2,1,0:T(1,128)S(1)}, s32[1,1,192]{2,1,0:T(1,128)}, u32[]{:S(2)}) copy-start(s32[1,1,192]{2,1,0:T(1,128)} %param.11) | copy-start | bytes 2308
  7.2 49.5 %copy-start.8 = (s32[1,4]{1,0:T(1,128)S(1)}, s32[1,4]{1,0:T(1,128)}, u32[]{:S(2)}) copy-start(s32[1,4]{1,0:T(1,128)} %param.13) | copy-start | bytes 52
  7.2 49.6 %copy-start.4 = (f32[1,32,128]{2,1,0:T(8,128)S(1)}, f32[1,32,128]{2,1,0:T(8,128)}, u32[]{:S(2)}) copy-start(f32[1,32,128]{2,1,0:T(8,128)} %param.15) | copy-start | bytes 49156
  7.2 54.9 %copy-start.5 = (f32[1,32,128]{2,1,0:T(8,128)S(1)}, f32[1,32,128]{2,1,0:T(8,128)}, u32[]{:S(2)}) copy-start(f32[1,32,128]{2,1,0:T(8,128)} %param.14) | copy-start | bytes 49156
  7.2 82.2 %all-reduce.5.cloned.1.call-start = ((), (), s32[]{:S(2)}) async-start(), calls=%async_computation | async-start | bytes 262144 | tf_op jit(solution)/shard_map/psum | solution.py:39
  42.6 53.6 %copy-start.7 = (s32[1,1,192]{2,1,0:T(1,128)S(1)}, s32[1,1,192]{2,1,0:T(1,128)}, u32[]{:S(2)}) copy-start(s32[1,1,192]{2,1,0:T(1,128)} %param.10) | copy-start | bytes 2308
  48.7 55.3 %copy-start.9 = (u32[32]{0:T(128)S(1)}, u32[32]{0:T(128)}, u32[]{:S(2)}) copy-start(u32[32]{0:T(128)} %constant.40) | copy-start | bytes 388
  48.7 126.7 %copy-start.2 = (f32[1,16,128]{2,1,0:T(8,128)S(1)}, f32[1,16,128]{2,1,0:T(8,128)}, u32[]{:S(2)}) copy-start(f32[1,16,128]{2,1,0:T(8,128)} %param.8) | copy-start | bytes 24580
  55.9 0.7 copy-start.1
  56.6 118.0 %all-reduce.7.cloned.1.call-start = ((), (), s32[]{:S(2)}) async-start(), calls=%async_computation.1 | async-start | bytes 262144
  103.3 0.7 copy-start
  175.4 0.6 copy-start.3
Sparse Core Ops, SparseCore 0:
  56.7 32.6 all-reduce.4
  104.1 70.4 all-reduce.6
where the time goes:
time: 183 us
  waiting for transfers between devices  91.6 us (50%)
  blocking collectives  42.9 us (23%)
  other arithmetic  16.5 us (9%)
  between operations  15.5 us (8%)
  matrix products  10.7 us (6%)
  local copies, waits for them, and re-layouts  5.65 us (3%)
    unnamed x3, waiting for transfers between devices  69.4 us
    all_gather x1, blocking collectives, on_device(): slab_image = lax.all_gather(own_image, 'view', axis=0, tiled=True)  32.4 us
    psum x1, waiting for transfers between devices, on_device(): totals = lax.psum(partial_rays, 'slab')  22.2 us
    scatter-add x1, other arithmetic, on_device(): jax.ops.segment_sum(products, ray_rows, num_segments=ray_total)  7.15 us
    scatter-add x1, other arithmetic, on_device(): jax.ops.segment_sum(back_products, pixel_rows, num_segments=voxel_total)  7.15 us
    dot_general x1, matrix products, on_device(): jnp.einsum('krv,kcv->kcr', local_tiles, operand, preferred_element_type=j...  6.14 us
    all_gather x1, blocking collectives, on_device(): lax.all_gather(sinogram[0], 'slab', axis=0, tiled=True)  5.24 us
    all_gather x1, blocking collectives, on_device(): lax.all_gather(weights[0], 'slab', axis=0, tiled=True)  5.24 us
  transfers between devices with their start and end apart: 2, of which 2 were waited for; matrix products, arithmetic and copies ran while one was open for 0% of the time, Pallas kernels for 0%

commit v1 on v0

--- a/solution.py
+++ b/solution.py
@@ -26,7 +26,12 @@
     voxel_total = volume.shape[1] * lax.axis_size("view")
     live_mask = (jnp.arange(local_tiles.shape[0], dtype=jnp.int32) < count_here).astype(jnp.float32)
     own_image = volume[0].astype(jnp.bfloat16)
-    slab_image = lax.all_gather(own_image, "view", axis=0, tiled=True)
+    ring = [own_image]
+    for hop in range(7):
+        ring.append(lax.ppermute(ring[-1], "view", [(dev, (dev + 1) % 8) for dev in range(8)]))
+    slab_image = jnp.roll(
+        jnp.concatenate(ring[::-1], axis=0), (lax.axis_index("view") + 1) * ring[0].shape[0], axis=0
+    )
     picked = slab_image[pixel_rows]
     operand = jnp.stack([picked, jnp.ones_like(picked)], axis=1)
     products = jnp.einsum("krv,kcv->kcr", local_tiles, operand, preferred_element_type=jnp.float32)

time: 183 us -> 193 us (1.055)
  waiting for transfers between devices: 91.6 us -> 129 us
  blocking collectives: 42.9 us -> 10.5 us
  starting transfers between devices: 0.08 us -> 3.06 us
  other arithmetic: 16.5 us -> 18.6 us
    ppermute x0 -> x7, waiting for transfers between devices: none -> 40.4 us  [on_device(): lax.ppermute(ring[-1], 'view', [(dev, (dev + 1) % 8) for dev in range(8)])]
    all_gather x1 -> x0, blocking collectives: 32.4 us -> none  [on_device(): slab_image = lax.all_gather(own_image, 'view', axis=0, tiled=True)]
    psum x1, waiting for transfers between devices: 22.2 us -> 18.8 us  [on_device(): totals = lax.psum(partial_rays, 'slab')]
    ppermute x0 -> x7, starting transfers between devices: none -> 2.98 us  [on_device(): lax.ppermute(ring[-1], 'view', [(dev, (dev + 1) % 8) for dev in range(8)])]
  transfers between devices with their start and end apart: 2 -> 9, of which waited for: 2 -> 9; matrix products, arithmetic and copies ran while one was open for 0% -> 1% of each run, Pallas kernels for 0% -> 0%
where the time goes in v1:
time: 193 us
  waiting for transfers between devices  129 us (67%)
  other arithmetic  18.6 us (10%)
  between operations  15.5 us (8%)
  matrix products  10.7 us (6%)
  blocking collectives  10.5 us (5%)
  local copies, waits for them, and re-layouts  5.75 us (3%)
  starting transfers between devices  3.06 us (2%)
    unnamed x3, waiting for transfers between devices  69.4 us
    ppermute x7, waiting for transfers between devices, on_device(): lax.ppermute(ring[-1], 'view', [(dev, (dev + 1) % 8) for dev in range(8)])  40.4 us
    psum x1, waiting for transfers between devices, on_device(): totals = lax.psum(partial_rays, 'slab')  18.8 us
    scatter-add x1, other arithmetic, on_device(): jax.ops.segment_sum(products, ray_rows, num_segments=ray_total)  7.15 us
    scatter-add x1, other arithmetic, on_device(): jax.ops.segment_sum(back_products, pixel_rows, num_segments=voxel_total)  7.15 us
    dot_general x1, matrix products, on_device(): jnp.einsum('krv,kcv->kcr', local_tiles, operand, preferred_element_type=j...  6.14 us
    all_gather x1, blocking collectives, on_device(): lax.all_gather(weights[0], 'slab', axis=0, tiled=True)  5.23 us
    all_gather x1, blocking collectives, on_device(): lax.all_gather(sinogram[0], 'slab', axis=0, tiled=True)  5.23 us
  transfers between devices with their start and end apart: 9, of which 9 were waited for; matrix products, arithmetic and copies ran while one was open for 1% of the time, Pallas kernels for 0%

profile of v1, /device:TPU:0, one launch (start us, length us, event | category | flops | bytes accessed | tf_op | source)
XLA Modules:
  0.0 192.7 jit_solution(15526632408230778195)
XLA Ops:
  7.2 0.0 copy-start.6
  7.2 0.0 copy-start.8
  7.2 0.0 copy-start.4
  7.2 0.0 copy-start.5
  7.2 0.0 all-reduce.5.cloned.1.call-start
  7.3 0.7 convert_bitcast_fusion
  8.0 3.0 %collective-permute-start = (bf16[16,128]{1,0:T(8,128)(2,1)S(1)}, bf16[16,128]{1,0:T(8,128)(2,1)S(1)}, u32[]{:S(2)}, u32[]{:S(2)}) collective-permute-start(bf16[16,128]{1,0:T(8,128)(2,1)S(1)} %convert_bitcast_fusion), channel_id=1, source_target_pairs={{0,4},{4,8},{8,12},{12,16},{16,20},{20,24},{24,28},{28,0},{1,5},{5... | collective-permute-start | bytes 12296 | tf_op jit(solution)/shard_map/ppermute | solution.py:31
  10.9 4.6 %collective-permute-done = bf16[16,128]{1,0:T(8,128)(2,1)S(1)} collective-permute-done((bf16[16,128]{1,0:T(8,128)(2,1)S(1)}, bf16[16,128]{1,0:T(8,128)(2,1)S(1)}, u32[]{:S(2)}, u32[]{:S(2)}) %collective-permute-start) | collective-permute-done | bytes 4128 | tf_op jit(solution)/shard_map/ppermute | solution.py:31
  15.5 0.0 collective-permute-start.1
  15.5 6.3 %collective-permute-done.1 = bf16[16,128]{1,0:T(8,128)(2,1)S(1)} collective-permute-done((bf16[16,128]{1,0:T(8,128)(2,1)S(1)}, bf16[16,128]{1,0:T(8,128)(2,1)S(1)}, u32[]{:S(2)}, u32[]{:S(2)}) %collective-permute-start.1) | collective-permute-done | bytes 4128 | tf_op jit(solution)/shard_map/ppermute | solution.py:31
  21.8 0.0 collective-permute-start.2
  21.9 0.7 compare_select_fusion
  22.5 5.6 %collective-permute-done.2 = bf16[16,128]{1,0:T(8,128)(2,1)S(1)} collective-permute-done((bf16[16,128]{1,0:T(8,128)(2,1)S(1)}, bf16[16,128]{1,0:T(8,128)(2,1)S(1)}, u32[]{:S(2)}, u32[]{:S(2)}) %collective-permute-start.2) | collective-permute-done | bytes 4128 | tf_op jit(solution)/shard_map/ppermute | solution.py:31
  28.2 0.0 collective-permute-start.3
  28.2 0.7 compare_select_fusion.1
  28.8 5.6 %collective-permute-done.3 = bf16[16,128]{1,0:T(8,128)(2,1)S(1)} collective-permute-done((bf16[16,128]{1,0:T(8,128)(2,1)S(1)}, bf16[16,128]{1,0:T(8,128)(2,1)S(1)}, u32[]{:S(2)}, u32[]{:S(2)}) %collective-permute-start.3) | collective-permute-done | bytes 4128 | tf_op jit(solution)/shard_map/ppermute | solution.py:31
  34.5 0.0 collective-permute-start.4
  35.1 5.6 %collective-permute-done.4 = bf16[16,128]{1,0:T(8,128)(2,1)S(1)} collective-permute-done((bf16[16,128]{1,0:T(8,128)(2,1)S(1)}, bf16[16,128]{1,0:T(8,128)(2,1)S(1)}, u32[]{:S(2)}, u32[]{:S(2)}) %collective-permute-start.4) | collective-permute-done | bytes 4128 | tf_op jit(solution)/shard_map/ppermute | solution.py:31
  40.8 0.0 collective-permute-start.5
  40.8 6.3 %collective-permute-done.5 = bf16[16,128]{1,0:T(8,128)(2,1)S(1)} collective-permute-done((bf16[16,128]{1,0:T(8,128)(2,1)S(1)}, bf16[16,128]{1,0:T(8,128)(2,1)S(1)}, u32[]{:S(2)}, u32[]{:S(2)}) %collective-permute-start.5) | collective-permute-done | bytes 4128 | tf_op jit(solution)/shard_map/ppermute | solution.py:31
  47.1 0.0 collective-permute-start.6
  47.1 6.3 %collective-permute-done.6 = bf16[16,128]{1,0:T(8,128)(2,1)S(1)} collective-permute-done((bf16[16,128]{1,0:T(8,128)(2,1)S(1)}, bf16[16,128]{1,0:T(8,128)(2,1)S(1)}, u32[]{:S(2)}, u32[]{:S(2)}) %collective-permute-start.6) | collective-permute-done | bytes 4128 | tf_op jit(solution)/shard_map/ppermute | solution.py:31
  53.4 0.7 constant_dynamic-update-slice_fusion.8
  54.2 0.7 constant_dynamic-update-slice_fusion
  54.9 0.8 gather_fusion
  55.7 0.1 copy.19
  55.8 0.0 copy-start.7
  55.8 6.1 %fusion.4 = f32[192,2,128]{2,1,0:T(2,128)S(1)} fusion(bf16[1,1,192,128,128]{4,3,2,1,0:T(8,128)(2,1)} %param.9, f32[192]{0:T(256)S(1)} %compare_convert_fusion, bf16[192,1,128]{2,1,0:T(2,128)(2,1)S(1)} %copy.19), kind=kOutput, calls=%fused_computation.8 | convolution fusion | flops 12632064 | bytes 6537984 | tf_op jit(solution)/shard_map/krv,kcv->kcr/dot_general | solution.py:37
  61.9 0.0 copy-start.9
  61.9 0.0 copy-start.2
  62.0 0.0 copy-done.6
  62.0 7.2 %scatter_fusion = f32[128,2,128]{2,1,0:T(2,128)S(1)} fusion(f32[128,2,128]{2,1,0:T(2,128)S(1)} %broadcast.75.clone, s32[192]{0:T(256)S(1)} %bitcast.72, f32[192,2,128]{2,1,0:T(2,128)S(1)} %fusion.4), kind=kCustom, calls=%fused_computation.2 | custom fusion | flops 49152 | bytes 590592 | tf_op jit(solution)/shard_map/scatter-add | solution.py:39
  69.1 0.0 copy-start.1
  69.2 0.6 copy-done.1
  69.8 0.0 all-reduce.5.cloned.1.call-update
  69.8 0.0 all-reduce.7.cloned.1.call-start
  69.9 0.0 copy-done.8
  69.9 0.1 compare_reduce_fusion
  70.0 0.0 copy-done.4
  70.0 5.2 %all-gather = f32[1,128,128]{2,1,0:T(8,128)S(1)} all-gather(f32[1,32,128]{2,1,0:T(8,128)S(1)} %copy-done.4), channel_id=2, replica_groups=mesh['view'=8,'slab'=4] {'slab'}, dimensions={1}, use_global_device_ids=true | all-gather | bytes 81920 | tf_op jit(solution)/shard_map/all_gather | solution.py:42
  75.2 0.0 copy-done.5
  75.2 5.2 %all-gather.1 = f32[1,128,128]{2,1,0:T(8,128)S(1)} all-gather(f32[1,32,128]{2,1,0:T(8,128)S(1)} %copy-done.5), channel_id=3, replica_groups=mesh['view'=8,'slab'=4] {'slab'}, dimensions={1}, use_global_device_ids=true | all-gather | bytes 81920 | tf_op jit(solution)/shard_map/all_gather | solution.py:41
  80.4 18.8 %all-reduce.5.cloned.1.call-done = f32[128,2,128]{2,1,0:T(2,128)} async-done(((f32[128,2,128]{2,1,0:T(2,128)}), f32[128,2,128]{2,1,0:T(2,128)}) %all-reduce.5.cloned.1.call-update) | async-done | bytes 131088 | tf_op jit(solution)/shard_map/psum | solution.py:44
  99.2 1.1 fusion.19
  100.3 0.1 fusion.14
  100.4 0.1 copy.21
  100.5 0.8 gather_fusion.1
  101.3 4.5 %fusion.7 = f32[192,2,128]{2,1,0:T(2,128)S(1)} fusion(bf16[192,2,128]{2,1,0:T(2,128)(2,1)S(1)} %gather_fusion.1, bf16[1,1,192,128,128]{4,3,2,1,0:T(8,128)(2,1)} %param.9, f32[192]{0:T(256)S(1)} %compare_convert_fusion), kind=kOutput, calls=%fused_computation.9 | convolution fusion | flops 12632064 | bytes 6587136 | tf_op jit(solution)/shard_map/krv,kcr->kcv/dot_general | solution.py:47
  105.9 0.0 copy-done.7
  105.9 7.1 %scatter_fusion.1 = f32[128,2,128]{2,1,0:T(2,128)S(1)} fusion(f32[128,2,128]{2,1,0:T(2,128)S(1)} %broadcast.75, s32[192]{0:T(256)S(1)} %bitcast.73, f32[192,2,128]{2,1,0:T(2,128)S(1)} %fusion.7), kind=kCustom, calls=%fused_computation.3 | custom fusion | flops 49152 | bytes 590592 | tf_op jit(solution)/shard_map/scatter-add | solution.py:51
  113.1 0.0 copy-start
  113.1 0.6 copy-done
  113.7 0.0 all-reduce.7.cloned.1.call-update
  113.8 0.0 copy-done.9
  113.8 0.6 dynamic-slice
  115.0 69.4 %all-reduce.7.cloned.1.call-done = f32[128,2,128]{2,1,0:T(2,128)} async-done(((f32[128,2,128]{2,1,0:T(2,128)}), f32[128,2,128]{2,1,0:T(2,128)}) %all-reduce.7.cloned.1.call-update) | async-done | bytes 131088
  184.4 0.8 constant_dynamic-slice_fusion
  185.2 0.0 copy-start.3
  185.2 0.0 copy-done.2
  185.2 0.6 fusion.17
  185.9 0.0 copy-done.3
  (22 shorter events, 0.2 us)
Async XLA Ops:
  7.2 54.8 %copy-start.6 = (s32[1,1,192]{2,1,0:T(1,128)S(1)}, s32[1,1,192]{2,1,0:T(1,128)}, u32[]{:S(2)}) copy-start(s32[1,1,192]{2,1,0:T(1,128)} %param.11) | copy-start | bytes 2308
  7.2 62.7 %copy-start.8 = (s32[1,4]{1,0:T(1,128)S(1)}, s32[1,4]{1,0:T(1,128)}, u32[]{:S(2)}) copy-start(s32[1,4]{1,0:T(1,128)} %param.13) | copy-start | bytes 52
  7.2 62.8 %copy-start.4 = (f32[1,32,128]{2,1,0:T(8,128)S(1)}, f32[1,32,128]{2,1,0:T(8,128)}, u32[]{:S(2)}) copy-start(f32[1,32,128]{2,1,0:T(8,128)} %param.15) | copy-start | bytes 49156
  7.2 68.0 %copy-start.5 = (f32[1,32,128]{2,1,0:T(8,128)S(1)}, f32[1,32,128]{2,1,0:T(8,128)}, u32[]{:S(2)}) copy-start(f32[1,32,128]{2,1,0:T(8,128)} %param.14) | copy-start | bytes 49156
  7.2 92.0 %all-reduce.5.cloned.1.call-start = ((), (), s32[]{:S(2)}) async-start(), calls=%async_computation | async-start | bytes 262144 | tf_op jit(solution)/shard_map/psum | solution.py:44
  8.0 7.6 %collective-permute-start = (bf16[16,128]{1,0:T(8,128)(2,1)S(1)}, bf16[16,128]{1,0:T(8,128)(2,1)S(1)}, u32[]{:S(2)}, u32[]{:S(2)}) collective-permute-start(bf16[16,128]{1,0:T(8,128)(2,1)S(1)} %convert_bitcast_fusion), channel_id=1, source_target_pairs={{0,4},{4,8},{8,12},{12,16},{16,20},{20,24},{24,28},{28,0},{1,5},{5... | collective-permute-start | bytes 12296 | tf_op jit(solution)/shard_map/ppermute | solution.py:31
  15.5 6.3 %collective-permute-start.1 = (bf16[16,128]{1,0:T(8,128)(2,1)S(1)}, bf16[16,128]{1,0:T(8,128)(2,1)S(1)}, u32[]{:S(2)}, u32[]{:S(2)}) collective-permute-start(bf16[16,128]{1,0:T(8,128)(2,1)S(1)} %collective-permute-done), channel_id=1, source_target_pairs={{0,4},{4,8},{8,12},{12,16},{16,20},{20,24},{24,28},{28,0},{1,5},{5... | collective-permute-start | bytes 12296 | tf_op jit(solution)/shard_map/ppermute | solution.py:31
  21.8 6.3 %collective-permute-start.2 = (bf16[16,128]{1,0:T(8,128)(2,1)S(1)}, bf16[16,128]{1,0:T(8,128)(2,1)S(1)}, u32[]{:S(2)}, u32[]{:S(2)}) collective-permute-start(bf16[16,128]{1,0:T(8,128)(2,1)S(1)} %collective-permute-done.1), channel_id=1, source_target_pairs={{0,4},{4,8},{8,12},{12,16},{16,20},{20,24},{24,28},{28,0},{1,5},{5... | collective-permute-start | bytes 12296 | tf_op jit(solution)/shard_map/ppermute | solution.py:31
  28.2 6.3 %collective-permute-start.3 = (bf16[16,128]{1,0:T(8,128)(2,1)S(1)}, bf16[16,128]{1,0:T(8,128)(2,1)S(1)}, u32[]{:S(2)}, u32[]{:S(2)}) collective-permute-start(bf16[16,128]{1,0:T(8,128)(2,1)S(1)} %collective-permute-done.2), channel_id=1, source_target_pairs={{0,4},{4,8},{8,12},{12,16},{16,20},{20,24},{24,28},{28,0},{1,5},{5... | collective-permute-start | bytes 12296 | tf_op jit(solution)/shard_map/ppermute | solution.py:31
  34.5 6.3 %collective-permute-start.4 = (bf16[16,128]{1,0:T(8,128)(2,1)S(1)}, bf16[16,128]{1,0:T(8,128)(2,1)S(1)}, u32[]{:S(2)}, u32[]{:S(2)}) collective-permute-start(bf16[16,128]{1,0:T(8,128)(2,1)S(1)} %collective-permute-done.3), channel_id=1, source_target_pairs={{0,4},{4,8},{8,12},{12,16},{16,20},{20,24},{24,28},{28,0},{1,5},{5... | collective-permute-start | bytes 12296 | tf_op jit(solution)/shard_map/ppermute | solution.py:31
  40.8 6.3 %collective-permute-start.5 = (bf16[16,128]{1,0:T(8,128)(2,1)S(1)}, bf16[16,128]{1,0:T(8,128)(2,1)S(1)}, u32[]{:S(2)}, u32[]{:S(2)}) collective-permute-start(bf16[16,128]{1,0:T(8,128)(2,1)S(1)} %collective-permute-done.4), channel_id=1, source_target_pairs={{0,4},{4,8},{8,12},{12,16},{16,20},{20,24},{24,28},{28,0},{1,5},{5... | collective-permute-start | bytes 12296 | tf_op jit(solution)/shard_map/ppermute | solution.py:31
  47.1 6.3 %collective-permute-start.6 = (bf16[16,128]{1,0:T(8,128)(2,1)S(1)}, bf16[16,128]{1,0:T(8,128)(2,1)S(1)}, u32[]{:S(2)}, u32[]{:S(2)}) collective-permute-start(bf16[16,128]{1,0:T(8,128)(2,1)S(1)} %collective-permute-done.5), channel_id=1, source_target_pairs={{0,4},{4,8},{8,12},{12,16},{16,20},{20,24},{24,28},{28,0},{1,5},{5... | collective-permute-start | bytes 12296 | tf_op jit(solution)/shard_map/ppermute | solution.py:31
  55.8 50.1 %copy-start.7 = (s32[1,1,192]{2,1,0:T(1,128)S(1)}, s32[1,1,192]{2,1,0:T(1,128)}, u32[]{:S(2)}) copy-start(s32[1,1,192]{2,1,0:T(1,128)} %param.10) | copy-start | bytes 2308
  61.9 51.8 %copy-start.9 = (u32[32]{0:T(128)S(1)}, u32[32]{0:T(128)}, u32[]{:S(2)}) copy-start(u32[32]{0:T(128)} %constant.70) | copy-start | bytes 388
  61.9 123.3 %copy-start.2 = (f32[1,16,128]{2,1,0:T(8,128)S(1)}, f32[1,16,128]{2,1,0:T(8,128)}, u32[]{:S(2)}) copy-start(f32[1,16,128]{2,1,0:T(8,128)} %param.8) | copy-start | bytes 24580
  69.1 0.6 copy-start.1
  69.8 114.6 %all-reduce.7.cloned.1.call-start = ((), (), s32[]{:S(2)}) async-start(), calls=%async_computation.1 | async-start | bytes 262144
  113.1 0.6 copy-start
  185.2 0.6 copy-start.3
Sparse Core Ops, SparseCore 0:
  69.9 29.2 all-reduce.4
  113.9 70.4 all-reduce.6
